TPU v7x, 256 devices: a whole 4x4x8 slice. The times are simulated.
256 devices in a mesh: pole: 8 (over y, x_lo), leaf: 32 (over x_hi, z, core).
Axes of the slice: x: 4 (x_hi: 2, x_lo: 2; x = x_hi * 2 + x_lo), y: 4, z: 8, core: 2. Of those that a mesh axis runs over, the one named last changes fastest.
Arguments:
- inverse_front: bfloat16 [8, 2, 8192, 8192], P('pole', None, 'leaf'), may hold values from -6 to 6
- factor_panel: bfloat16 [8, 8192, 512], P('pole', 'leaf'), may hold values from -0.0625 to 0.0625
- diag_inverse: bfloat16 [8, 256, 512], P('pole'), may hold values from -6 to 6
- pole_weight: float32 [8, 2], P('pole'), may hold values from -2.4 to 2.4
- structure: int32 [32], replicated, may hold values from 0 to 1, as said below
- block_owner: int32 [1024, 1], P('leaf'), may hold values from 0 to 31; in each aligned block of 32 rows (0 to 31, 32 to 63, ...) at most 2 rows name the same one
Outputs:
- owned_density: float32 [2048, 8, 256], P('leaf')
- diag_density: float32 [256, 256], replicated
Inputs may be any that keep to these rules, and one draw needn't show every extreme that they name: `structure`: exactly 16 entries are 1. `block_owner`: among the 32 blocks of one index of leaf no owner appears more than 2 times, and in some index's blocks one owner appears exactly 2 times.
All inputs are finite; a program needn't handle non-finite values.
Results may differ from a plain program's by a relative error of at most 0.0003.
Values may be sent and summed in bfloat16 or wider, within the bound.
No kernel may reach another device: no remote copies, remote signals or barrier semaphores. Data moves between devices by JAX's collectives and lax.ppermute only.
A program may use at most 64 MiB of HBM per device.

v0:
```python
import jax
import jax.numpy as jnp
from jax import lax
from jax.sharding import PartitionSpec as P


def kept_rows(structure, first_row, row_count, block_width):
    block_ids = jnp.arange(structure.shape[0], dtype=jnp.int32)
    which_block = (first_row + jnp.arange(row_count, dtype=jnp.int32)) // block_width
    matches = which_block[:, None] == block_ids[None, :]
    return jnp.sum(jnp.where(matches, structure[None, :], 0), axis=1).astype(jnp.float32)


def panel_product(columns, panel):
    return jnp.einsum("pcrk,pkn->pcrn", columns, panel, preferred_element_type=jnp.float32)


def body(inverse_front, factor_panel, diag_inverse, pole_weight, structure, block_owner):
    leaves = lax.axis_size("leaf")
    rows_here = inverse_front.shape[2]
    block_width = factor_panel.shape[2] // 2
    first_row = lax.axis_index("leaf") * rows_here
    panel_rows = lax.all_gather(factor_panel, "leaf", axis=1, tiled=True)
    row_count = panel_rows.shape[1]
    keep_piece = kept_rows(structure, jnp.int32(0), row_count, block_width).astype(jnp.bfloat16)
    masked = panel_rows * keep_piece[None, :, None]
    product = panel_product(inverse_front, masked)
    keep_here = kept_rows(structure, first_row, rows_here, block_width)[None, :, None]
    block_real = -(product[:, 0, :, :block_width] - product[:, 1, :, block_width:]) * keep_here
    block_imag = -(product[:, 0, :, block_width:] + product[:, 1, :, :block_width]) * keep_here
    weight_real = pole_weight[:, 0][:, None, None]
    weight_imag = pole_weight[:, 1][:, None, None]
    density_part = jnp.sum(weight_real * block_imag + weight_imag * block_real, axis=0)
    panel_kept = factor_panel.astype(jnp.float32) * keep_here
    panel_real = panel_kept[:, :, :block_width]
    panel_imag = panel_kept[:, :, block_width:]
    precise = lax.Precision.HIGHEST

    def transposed(left_side, right_side):
        return jnp.einsum("prk,prn->pkn", left_side, right_side, precision=precise)

    schur_real = transposed(panel_real, block_real) - transposed(panel_imag, block_imag)
    schur_imag = transposed(panel_real, block_imag) + transposed(panel_imag, block_real)
    diag_full = diag_inverse.astype(jnp.float32)
    schur_real, schur_imag = lax.psum((schur_real, schur_imag), "leaf")
    corner_real = diag_full[:, :, :block_width] - schur_real
    corner_imag = diag_full[:, :, block_width:] - schur_imag
    corner_terms = jnp.sum(weight_real * corner_imag + weight_imag * corner_real, axis=0)
    diag_density = lax.psum(corner_terms, "pole")
    blocks_mine = block_owner.shape[0]
    element_rows = rows_here // blocks_mine
    capacity = max(2, (2 * blocks_mine + leaves - 1) // leaves)
    owners = block_owner[:, 0]
    one_hot = (owners[:, None] == jnp.arange(leaves, dtype=jnp.int32)[None, :]).astype(jnp.int32)
    ranks = jnp.sum((jnp.cumsum(one_hot, axis=0) - one_hot) * one_hot, axis=1)
    slot_index = owners * capacity + ranks
    density_rows = lax.psum(density_part, "pole")
    column_count = density_rows.shape[1]
    element_blocks = density_rows.reshape(blocks_mine, element_rows, column_count)
    buffer_zero = jnp.zeros((leaves * capacity, element_rows, column_count), jnp.float32)
    owned_density = lax.all_to_all(
        buffer_zero.at[slot_index].set(element_blocks),
        "leaf",
        split_axis=0,
        concat_axis=0,
        tiled=True,
    )
    return (owned_density, diag_density)


def solution(mesh):
    placed = (
        P("pole", None, "leaf", None),
        P("pole", "leaf", None),
        P("pole", None, None),
        P("pole", None),
        P(),
        P("leaf", None),
    )
    return jax.shard_map(
        body, mesh=mesh, in_specs=placed, out_specs=(P("leaf", None, None), P()), check_vma=False
    )
```

profile of v0, /device:TPU:1, one launch (start us, length us, event | category | flops | bytes accessed | tf_op | source)
XLA Modules:
  0.0 519.0 jit_solution(18408811787066555844)
XLA Ops:
  7.2 0.0 all-gather.2.cloned.1.call-start
  7.2 0.7 all-gather.2.cloned.1.call-update
  7.9 0.0 all-reduce.5.cloned.1.call-start
  8.0 0.7 select_reduce_fusion.1
  8.7 0.9 select_reduce_fusion
  9.6 1.1 convert_multiply_fusion
  10.7 0.0 copy-start
  10.7 0.0 copy-start.2
  10.7 0.0 copy-start.1
  10.7 105.5 %all-gather.2.cloned.1.call-done = bf16[1,8192,512]{2,1,0:T(8,128)(2,1)} async-done(((bf16[1,256,512]{2,1,0:T(8,128)(2,1)}), bf16[1,8192,512]{2,1,0:T(8,128)(2,1)}) %all-gather.2.cloned.1.call-update) | async-done | bytes 8388624 | tf_op jit(solution)/shard_map/all_gather | solution.py:23
  116.2 10.4 %fusion.5 = f32[1,2,256,512]{3,2,1,0:T(8,128)S(1)} fusion(bf16[1,2,256,8192]{3,2,1,0:T(8,128)(2,1)} %param.6, bf16[1,8192,512]{2,1,0:T(8,128)(2,1)} %all-gather.2.cloned.1.call-done, bf16[8192]{0:T(1024)(128)(2,1)S(1)} %convert_convert_fusion), kind=kOutput, calls=%fused_computation.6 | convolution fusion | flops 4311744512 | bytes 17842176 | tf_op jit(solution)/shard_map/pcrk,pkn->pcrn/dot_general | solution.py:15
  126.6 0.7 fusion.18
  127.2 0.7 fusion.22
  127.9 1.4 fusion.10
  129.3 1.4 fusion.11
  130.7 0.0 all-reduce.5.cloned.1.call-update
  130.7 0.0 all-reduce.7.cloned.1.call-start
  130.7 0.0 copy-done
  130.8 0.1 convert_element_type.34
  130.8 0.6 fusion.41
  131.4 2.0 fusion.26
  133.4 262.7 %all-reduce.5.cloned.1.call-done = (f32[1,256,256]{2,1,0:T(8,128)}, f32[1,256,256]{2,1,0:T(8,128)}) async-done(((f32[1,256,256]{2,1,0:T(8,128)}, f32[1,256,256]{2,1,0:T(8,128)}), (f32[1,256,256]{2,1,0:T(8,128)}, f32[1,256,256]{2,1,0:T(8,128)})) %all-reduce.5.cloned.1.call-update) | async-done | bytes 524304 | tf_op jit(solution)/shard_map/psum | solution.py:45
  396.1 3.0 fusion.14
  399.1 0.0 all-reduce.7.cloned.1.call-update
  399.2 0.1 fusion.35
  399.3 0.1 reduce_window_sum.11
  399.3 0.2 select_reduce_fusion.2
  399.5 74.7 %all-reduce.7.cloned.1.call-done = (f32[32,8,256]{2,1,0:T(8,128)}, f32[256,256]{1,0:T(8,128)}) async-done(((f32[32,8,256]{2,1,0:T(8,128)}, f32[256,256]{1,0:T(8,128)}), (f32[32,8,256]{2,1,0:T(8,128)}, f32[256,256]{1,0:T(8,128)})) %all-reduce.7.cloned.1.call-update) | async-done | bytes 524304 | tf_op jit(solution)/shard_map/psum | solution.py:57
  474.3 2.8 scatter_fusion
  477.1 32.8 %all_to_all.5 = f32[64,8,256]{2,1,0:T(8,128)S(1)} all-to-all(f32[64,8,256]{2,1,0:T(8,128)S(1)} %scatter_fusion), channel_id=1, replica_groups=mesh['pole'=8,'leaf'=32] {'leaf'}, dimensions={0} | all-to-all | bytes 1048576 | tf_op jit(solution)/shard_map/all_to_all | solution.py:61
  510.0 0.8 copy.14
  510.8 1.7 copy.15
  (8 shorter events, 0.1 us)
Async XLA Ops:
  7.2 109.0 %all-gather.2.cloned.1.call-start = ((), (), s32[]{:S(2)}) async-start(), calls=%async_computation.1 | async-start | bytes 8650752 | tf_op jit(solution)/shard_map/all_gather | solution.py:23
  7.9 388.2 %all-reduce.5.cloned.1.call-start = ((), (), s32[]{:S(2)}) async-start(), calls=%async_computation.2 | async-start | bytes 1048576 | tf_op jit(solution)/shard_map/psum | solution.py:45
  10.7 120.0 %copy-start = (bf16[1,256,512]{2,1,0:T(8,128)(2,1)S(1)}, bf16[1,256,512]{2,1,0:T(8,128)(2,1)}, u32[]{:S(2)}) copy-start(bf16[1,256,512]{2,1,0:T(8,128)(2,1)} %param.8) | copy-start | bytes 786436
  10.7 120.1 %copy-start.2 = (f32[1,2]{1,0:T(1,128)S(1)}, f32[1,2]{1,0:T(1,128)}, u32[]{:S(2)}) copy-start(f32[1,2]{1,0:T(1,128)} %param.9) | copy-start | bytes 28
  10.7 388.4 %copy-start.1 = (s32[32,1]{0,1:T(1,128)S(1)}, s32[32,1]{0,1:T(1,128)}, u32[]{:S(2)}) copy-start(s32[32,1]{0,1:T(1,128)} %param.11) | copy-start | bytes 388
  130.7 343.5 %all-reduce.7.cloned.1.call-start = ((), (), s32[]{:S(2)}) async-start(), calls=%async_computation.3 | async-start | bytes 1048576 | tf_op jit(solution)/shard_map/psum | solution.py:57
Sparse Core Ops, SparseCore 0:
  10.7 105.4 all-gather.1
  130.8 265.2 all-reduce.4
  399.4 74.7 all-reduce.6
where the time goes:
time: 519 us
  waiting for transfers between devices  444 us (86%)
  blocking collectives  32.8 us (6%)
  matrix products  14.4 us (3%)
  between operations  13.9 us (3%)
  other arithmetic  8.1 us (2%)
  local copies, waits for them, and re-layouts  5.93 us (1%)
    psum x1, waiting for transfers between devices, body(): schur_real, schur_imag = lax.psum((schur_real, schur_imag), 'leaf')  263 us
    all_gather x1, waiting for transfers between devices, body(): panel_rows = lax.all_gather(factor_panel, 'leaf', axis=1, tiled=True)  105 us
    psum x1, waiting for transfers between devices, body(): density_rows = lax.psum(density_part, 'pole')  74.7 us
    all_to_all x1, blocking collectives, body(): lax.all_to_all(buffer_zero.at[slot_index].set(element_blocks), 'leaf', sp...  32.8 us
  transfers between devices with their start and end apart: 3, of which 3 were waited for; matrix products, arithmetic and copies ran while one was open for 1% of the time, Pallas kernels for 0%

commit v1 on v0

--- a/solution.py
+++ b/solution.py
@@ -20,7 +20,7 @@
     rows_here = inverse_front.shape[2]
     block_width = factor_panel.shape[2] // 2
     first_row = lax.axis_index("leaf") * rows_here
-    panel_rows = lax.all_gather(factor_panel, "leaf", axis=1, tiled=True)
+    panel_rows = jnp.concatenate(lax.all_gather(factor_panel, "leaf"), axis=1)
     row_count = panel_rows.shape[1]
     keep_piece = kept_rows(structure, jnp.int32(0), row_count, block_width).astype(jnp.bfloat16)
     masked = panel_rows * keep_piece[None, :, None]

time: 519 us -> 521 us (level)
  no operation moved by 1% of the time
where the time goes in v1:
time: 521 us
  waiting for transfers between devices  444 us (85%)
  blocking collectives  32.8 us (6%)
  between operations  13.9 us (3%)
  other arithmetic  12.8 us (2%)
  matrix products  11.1 us (2%)
  local copies, waits for them, and re-layouts  5.94 us (1%)
    psum x1, waiting for transfers between devices, body(): schur_real, schur_imag = lax.psum((schur_real, schur_imag), 'leaf')  263 us
    all_gather x1, waiting for transfers between devices, body(): panel_rows = jnp.concatenate(lax.all_gather(factor_panel, 'leaf'), axis=1)  105 us
    psum x1, waiting for transfers between devices, body(): density_rows = lax.psum(density_part, 'pole')  74.7 us
    all_to_all x1, blocking collectives, body(): lax.all_to_all(buffer_zero.at[slot_index].set(element_blocks), 'leaf', sp...  32.8 us
  transfers between devices with their start and end apart: 3, of which 3 were waited for; matrix products, arithmetic and copies ran while one was open for 1% of the time, Pallas kernels for 0%

profile of v1, /device:TPU:1, one launch (start us, length us, event | category | flops | bytes accessed | tf_op | source)
XLA Modules:
  0.0 520.8 jit_solution(2770347157786636679)
XLA Ops:
  7.2 0.0 all-gather.3.cloned.1.call-start
  7.2 0.7 all-gather.3.cloned.1.call-update
  7.9 0.0 all-reduce.5.cloned.1.call-start
  8.0 0.7 select_reduce_fusion.1
  8.7 0.9 select_reduce_fusion
  9.7 1.1 convert_multiply_fusion
  10.7 105.5 %all-gather.3.cloned.1.call-done = bf16[32,256,512]{2,1,0:T(8,128)(2,1)} async-done(((bf16[1,256,512]{2,1,0:T(8,128)(2,1)}), bf16[32,256,512]{2,1,0:T(8,128)(2,1)}) %all-gather.3.cloned.1.call-update) | async-done | bytes 8388624 | tf_op jit(solution)/shard_map/all_gather | solution.py:23
  116.2 4.7 bitcast_multiply_fusion
  120.9 0.0 copy-start
  120.9 0.0 copy-start.2
  120.9 0.0 copy-start.1
  120.9 7.0 %fusion.2 = f32[1,2,256,512]{3,2,1,0:T(8,128)S(1)} fusion(bf16[8192,512,1]{1,0,2:T(8,128)(2,1)S(1)} %bitcast.81, bf16[1,2,256,8192]{3,2,1,0:T(8,128)(2,1)} %param.6), kind=kOutput, calls=%fused_computation.4 | convolution fusion | flops 4294967296 | bytes 17825792 | tf_op jit(solution)/shard_map/pcrk,pkn->pcrn/dot_general | solution.py:15
  128.0 0.7 fusion.13
  128.6 0.7 fusion.17
  129.3 1.4 fusion.5
  130.7 1.4 fusion.6
  132.1 0.0 all-reduce.5.cloned.1.call-update
  132.1 0.0 all-reduce.7.cloned.1.call-start
  132.1 0.1 convert_element_type.39
  132.2 0.6 fusion.36
  132.8 2.0 fusion.21
  134.8 263.2 %all-reduce.5.cloned.1.call-done = (f32[1,256,256]{2,1,0:T(8,128)}, f32[1,256,256]{2,1,0:T(8,128)}) async-done(((f32[1,256,256]{2,1,0:T(8,128)}, f32[1,256,256]{2,1,0:T(8,128)}), (f32[1,256,256]{2,1,0:T(8,128)}, f32[1,256,256]{2,1,0:T(8,128)})) %all-reduce.5.cloned.1.call-update) | async-done | bytes 524304 | tf_op jit(solution)/shard_map/psum | solution.py:45
  398.0 3.0 fusion.9
  401.0 0.0 all-reduce.7.cloned.1.call-update
  401.0 0.1 fusion.30
  401.1 0.1 reduce_window_sum.11
  401.1 0.2 select_reduce_fusion.2
  401.3 74.7 %all-reduce.7.cloned.1.call-done = (f32[32,8,256]{2,1,0:T(8,128)}, f32[256,256]{1,0:T(8,128)}) async-done(((f32[32,8,256]{2,1,0:T(8,128)}, f32[256,256]{1,0:T(8,128)}), (f32[32,8,256]{2,1,0:T(8,128)}, f32[256,256]{1,0:T(8,128)})) %all-reduce.7.cloned.1.call-update) | async-done | bytes 524304 | tf_op jit(solution)/shard_map/psum | solution.py:57
  476.1 2.8 scatter_fusion
  478.9 32.8 %all_to_all.5 = f32[64,8,256]{2,1,0:T(8,128)S(1)} all-to-all(f32[64,8,256]{2,1,0:T(8,128)S(1)} %scatter_fusion), channel_id=1, replica_groups=mesh['pole'=8,'leaf'=32] {'leaf'}, dimensions={0} | all-to-all | bytes 1048576 | tf_op jit(solution)/shard_map/all_to_all | solution.py:61
  511.8 0.8 copy.14
  512.6 1.7 copy.15
  (10 shorter events, 0.1 us)
Async XLA Ops:
  7.2 109.0 %all-gather.3.cloned.1.call-start = ((), (), s32[]{:S(2)}) async-start(), calls=%async_computation.1 | async-start | bytes 8650752 | tf_op jit(solution)/shard_map/all_gather | solution.py:23
  7.9 390.1 %all-reduce.5.cloned.1.call-start = ((), (), s32[]{:S(2)}) async-start(), calls=%async_computation.2 | async-start | bytes 1048576 | tf_op jit(solution)/shard_map/psum | solution.py:45
  120.9 11.3 %copy-start = (bf16[1,256,512]{2,1,0:T(8,128)(2,1)S(1)}, bf16[1,256,512]{2,1,0:T(8,128)(2,1)}, u32[]{:S(2)}) copy-start(bf16[1,256,512]{2,1,0:T(8,128)(2,1)} %param.8) | copy-start | bytes 786436
  120.9 11.3 %copy-start.2 = (f32[1,2]{1,0:T(1,128)S(1)}, f32[1,2]{1,0:T(1,128)}, u32[]{:S(2)}) copy-start(f32[1,2]{1,0:T(1,128)} %param.9) | copy-start | bytes 28
  120.9 280.1 %copy-start.1 = (s32[32,1]{0,1:T(1,128)S(1)}, s32[32,1]{0,1:T(1,128)}, u32[]{:S(2)}) copy-start(s32[32,1]{0,1:T(1,128)} %param.11) | copy-start | bytes 388
  132.1 344.0 %all-reduce.7.cloned.1.call-start = ((), (), s32[]{:S(2)}) async-start(), calls=%async_computation.3 | async-start | bytes 1048576 | tf_op jit(solution)/shard_map/psum | solution.py:57
Sparse Core Ops, SparseCore 0:
  10.7 105.4 all-gather.2
  132.2 265.7 all-reduce.4
  401.2 74.7 all-reduce.6
